TPU v7x, 128 devices: a whole 4x4x4 slice. The times are simulated.
128 devices in a mesh: dp: 4 (over x_lo, core), seq: 32 (over y, x_hi, z).
Axes of the slice: x: 4 (x_hi: 2, x_lo: 2; x = x_hi * 2 + x_lo), y: 4, z: 4, core: 2. Of those that a mesh axis runs over, the one named last changes fastest.
Arguments:
- embeddings: bfloat16 [4, 32, 512, 8192], P('dp', 'seq'), may hold values from -6 to 6
- layout: int32 [4, 32, 32], P('dp'), may hold values from 0 to 31, as said below
- lengths: int32 [4], P('dp'), may hold values from 4096 to 16384, as said below
- targets: int32 [4, 4096, 2048], P('dp', 'seq'), may hold values from 0 to 7
- projection: bfloat16 [8192, 768], P('dp'), may hold values from -0.0625 to 0.0625
- kernels: bfloat16 [2, 3, 768, 384], replicated, may hold values from -0.125 to 0.125
- mixers: bfloat16 [2, 384, 768], replicated, may hold values from -0.3125 to 0.3125
- readout: bfloat16 [768, 2048], replicated, may hold values from -0.21875 to 0.21875
Outputs:
- kernel_grads: float32 [2, 3, 768, 384], P(None, None, 'seq', 'dp')
- mixer_grads: float32 [2, 384, 768], P(None, 'seq', 'dp')
- readout_grad: float32 [768, 2048], P('seq', 'dp')
- trunk_grad: float32 [4, 8192, 768], P('dp', 'seq')
Inputs may be any that keep to these rules, and one draw needn't show every extreme that they name: For every window w and shard j, layout[w, s, j] over all shards s lists every block number once. `lengths`: multiples of 128; in every draw one window has the full 16384 and another the least.
All inputs are finite; a program needn't handle non-finite values.
Results may differ from a plain program's by a relative error of at most 0.017.
Values may be sent and summed in bfloat16 or wider, within the bound.
A program may use at most 128 MiB of HBM per device.

v0:
```python
import math
import jax
import jax.numpy as jnp
from jax import lax
from jax.sharding import PartitionSpec as P

SPREAD_FINE = 256
SPREAD_COARSE = 128


def with_halo(shard, sides, width):
    for axis, dim in sides:
        size, length = (lax.axis_size(axis), shard.shape[dim])
        up = [(i, (i + 1) % size) for i in range(size - 1)]
        down = [(j, i) for i, j in up]
        last = lax.slice_in_dim(shard, length - width, length, axis=dim)
        leading = lax.slice_in_dim(shard, 0, width, axis=dim)
        before = lax.ppermute(last, axis, up)
        after = lax.ppermute(leading, axis, down)
        shard = jnp.concatenate([before, shard, after], axis=dim)
    return shard


def gelu_exact(values):
    return 0.5 * values * (1.0 + lax.erf(values * (1.0 / math.sqrt(2.0))))


def gelu_slope(values):
    cumulative = 0.5 * (1.0 + lax.erf(values * (1.0 / math.sqrt(2.0))))
    density = jnp.exp(-0.5 * values * values) * (1.0 / math.sqrt(2.0 * math.pi))
    return cumulative + values * density


def matmul(left_side, right_side):
    return jnp.dot(left_side, right_side, preferred_element_type=jnp.float32)


def times_transposed(left_side, right_side):
    return lax.dot_general(
        left_side, right_side, (((1,), (1,)), ((), ())), preferred_element_type=jnp.float32
    )


def transposed_times(left_side, right_side):
    return lax.dot_general(
        left_side, right_side, (((0,), (0,)), ((), ())), preferred_element_type=jnp.float32
    )


def spread_taps(extended, spread, row_count):
    return (
        extended[0:row_count],
        extended[spread : spread + row_count],
        extended[2 * spread : 2 * spread + row_count],
    )


def block_rest(hidden, shifted, kernel, mixing):
    inner_sum = (
        matmul(shifted[0], kernel[0])
        + matmul(shifted[1], kernel[1])
        + matmul(shifted[2], kernel[2])
    )
    gated_out = gelu_exact(inner_sum).astype(jnp.bfloat16)
    output = hidden.astype(jnp.float32) + matmul(gated_out, mixing)
    pooled = (output.reshape(-1, 2, output.shape[1]).sum(axis=1) * 0.5).astype(jnp.bfloat16)
    return (pooled, inner_sum, gated_out)


def block_backward(upstream, shifted, inner_sum, gated_out, mixing):
    mixing_grad = transposed_times(gated_out, upstream)
    inner_grad = (times_transposed(upstream, mixing) * gelu_slope(inner_sum)).astype(jnp.bfloat16)
    kernel_grad = jnp.stack(
        [transposed_times(shifted[tap_index], inner_grad) for tap_index in range(3)]
    )
    return (kernel_grad, mixing_grad, inner_grad)


def shards(embeddings, layout, lengths, targets, projection, kernels, mixers, readout):
    groups = lax.axis_size("seq")
    windows_total = lax.axis_size("dp")
    device = lax.axis_index("seq")
    local_rows = embeddings[0, 0]
    row_count = local_rows.shape[0]
    block_rows = row_count // groups
    channels = projection.shape[1]
    layout_table = layout[0]
    length = lengths[0]
    shard_ids = jnp.arange(groups, dtype=jnp.int32)
    own_column = lax.dynamic_index_in_dim(layout_table, device, axis=1, keepdims=False)
    matches = (own_column[:, None] == shard_ids[None, :]).astype(jnp.int32)
    source_index = jnp.sum(shard_ids[:, None] * matches, axis=0)
    row_ids = jnp.arange(row_count, dtype=jnp.int32)
    owner_shard = row_ids // block_rows
    own_slots = lax.dynamic_index_in_dim(layout_table, device, axis=0, keepdims=False)
    source_position = (
        owner_shard * row_count
        + jnp.take(own_slots, owner_shard) * block_rows
        + row_ids % block_rows
    )
    inside = (source_position < length).astype(jnp.float32)
    outgoing = (
        jnp.dot(
            local_rows,
            lax.all_gather(projection, "dp", axis=0, tiled=True),
            preferred_element_type=jnp.float32,
        )
        * inside[:, None]
    ).astype(jnp.bfloat16)
    received = lax.all_to_all(
        outgoing.reshape(groups, block_rows, channels),
        "seq",
        split_axis=0,
        concat_axis=0,
        tiled=True,
    )
    hidden = jnp.take(received, source_index, axis=0).reshape(row_count, channels)
    fine_spread = SPREAD_FINE
    coarse_spread = SPREAD_COARSE
    half_count = row_count // 2
    fine_active = gelu_exact(hidden.astype(jnp.float32)).astype(jnp.bfloat16)
    fine_wide = with_halo(fine_active, (("seq", 0),), fine_spread)
    fine_shifted = spread_taps(fine_wide, fine_spread, row_count)
    first_pooled, fine_inner, fine_gated = block_rest(hidden, fine_shifted, kernels[0], mixers[0])
    coarse_active = gelu_exact(first_pooled.astype(jnp.float32)).astype(jnp.bfloat16)
    coarse_wide = with_halo(coarse_active, (("seq", 0),), coarse_spread)
    coarse_shifted = spread_taps(coarse_wide, coarse_spread, half_count)
    second, coarse_inner, coarse_gated = block_rest(
        first_pooled, coarse_shifted, kernels[1], mixers[1]
    )
    bin_count = row_count // 4
    logits = matmul(second, readout)
    bin_ids = device * bin_count + jnp.arange(bin_count, dtype=jnp.int32)
    valid_bins = (bin_ids * 4 < length).astype(jnp.float32)
    loss_scale = 2.0 / math.sqrt(windows_total * groups * bin_count)
    target_values = targets[0].astype(jnp.float32)
    logit_grad = (
        loss_scale
        * valid_bins[:, None]
        * (jax.nn.softplus(logits) - target_values)
        * jax.nn.sigmoid(logits)
    ).astype(jnp.bfloat16)
    readout_grad = transposed_times(second, logit_grad)
    upper_grad = (times_transposed(logit_grad, readout) * 0.5).astype(jnp.bfloat16)
    upper_rows = jnp.repeat(upper_grad, 2, axis=0)
    coarse_kernel, coarse_mixing, coarse_grad = block_backward(
        upper_rows, coarse_shifted, coarse_inner, coarse_gated, mixers[1]
    )
    grad_wide = with_halo(coarse_grad, (("seq", 0),), coarse_spread)
    input_grad = (
        times_transposed(
            grad_wide[2 * coarse_spread : 2 * coarse_spread + half_count], kernels[1][0]
        )
        + times_transposed(coarse_grad, kernels[1][1])
        + times_transposed(grad_wide[0:half_count], kernels[1][2])
    )
    first_grad = upper_rows.astype(jnp.float32) + input_grad * gelu_slope(
        first_pooled.astype(jnp.float32)
    )
    trunk_grad = first_grad * (math.sqrt(windows_total * groups * bin_count) * 0.5)
    lower_grad = (first_grad * 0.5).astype(jnp.bfloat16)
    lower_rows = jnp.repeat(lower_grad, 2, axis=0)
    fine_kernel, fine_mixing, fine_grad = block_backward(
        lower_rows, fine_shifted, fine_inner, fine_gated, mixers[0]
    )
    kernel_terms = jnp.stack([fine_kernel, coarse_kernel])
    mixer_terms = jnp.stack([fine_mixing, coarse_mixing])
    kernel_part, mixer_part, readout_part = (
        lax.psum_scatter(
            kernel_terms.astype(jnp.bfloat16), "seq", scatter_dimension=2, tiled=True
        ).astype(jnp.float32),
        lax.psum_scatter(
            mixer_terms.astype(jnp.bfloat16), "seq", scatter_dimension=1, tiled=True
        ).astype(jnp.float32),
        lax.psum_scatter(
            readout_grad.astype(jnp.bfloat16), "seq", scatter_dimension=0, tiled=True
        ).astype(jnp.float32),
    )
    kernel_total, mixer_total, readout_total = (
        lax.psum_scatter(
            kernel_part.astype(jnp.bfloat16), "dp", scatter_dimension=3, tiled=True
        ).astype(jnp.float32),
        lax.psum_scatter(
            mixer_part.astype(jnp.bfloat16), "dp", scatter_dimension=2, tiled=True
        ).astype(jnp.float32),
        lax.psum_scatter(
            readout_part.astype(jnp.bfloat16), "dp", scatter_dimension=1, tiled=True
        ).astype(jnp.float32),
    )
    return (kernel_total, mixer_total, readout_total, trunk_grad[None])


def solution(mesh):
    placed = (
        P("dp", "seq", None, None),
        P("dp", None, None),
        P("dp"),
        P("dp", "seq", None),
        P("dp", None),
        P(),
        P(),
        P(),
    )
    return jax.shard_map(
        shards,
        mesh=mesh,
        in_specs=placed,
        out_specs=(
            P(None, None, "seq", "dp"),
            P(None, "seq", "dp"),
            P("seq", "dp"),
            P("dp", "seq", None),
        ),
        check_vma=False,
    )
```

profile of v0, /device:TPU:1, one launch (start us, length us, event | category | flops | bytes accessed | tf_op | source)
XLA Modules:
  0.0 1127.8 jit_solution(4078228910551584165)
XLA Ops:
  11.2 4.3 compare_select_fusion.2
  15.5 15.7 %fusion.98 = f32[512]{0:T(512)S(1)} fusion(pred[512]{0:T(512)(128)(4,1)S(1)} %compare_reduce_fusion, pred[512]{0:T(512)(128)(4,1)S(1)} %compare_reduce_fusion.1, pred[512]{0:T(512)(128)(4,1)S(1)} %compare_reduce_fusion.2, pred[512]{0:T(512)(128)(4,1)S(1)} %compare_reduce_fusion.3, pred[512]{0:T(512)(128)(4,1)S(1)} %compare_reduce_fusion.4, ...), kind=kLoop, calls=%fused_computation.194 | loop fusion | flops 25600 | bytes 17000 | tf_op jit(solution)/shard_map/convert_element_type | solution.py:101
  31.2 98.4 %all-gather.2.cloned.1.call-done = bf16[8192,768]{1,0:T(8,128)(2,1)} async-done(((bf16[2048,768]{1,0:T(8,128)(2,1)}), bf16[8192,768]{1,0:T(8,128)(2,1)}) %all-gather.2.cloned.1.call-update) | async-done | bytes 12582928 | tf_op jit(solution)/shard_map/all_gather | solution.py:105
  129.6 13.4 %fusion.13 = bf16[512,768]{1,0:T(8,128)(2,1)} fusion(bf16[8192,768]{1,0:T(8,128)(2,1)} %all-gather.2.cloned.1.call-done, bf16[1,1,512,8192]{3,2,1,0:T(8,128)(2,1)} %param.8, f32[512]{0:T(512)S(1)} %fusion.98), kind=kOutput, calls=%fused_computation.29 | convolution fusion | flops 6443237376 | bytes 21760000 | tf_op jit(solution)/shard_map/dot_general | solution.py:103
  143.0 9.2 all-to-all-start
  152.6 14.5 %all-to-all-done = bf16[32,16,768]{2,1,0:T(8,128)(2,1)} async-done(((bf16[32,16,768]{2,1,0:T(8,128)(2,1)}), bf16[32,16,768]{2,1,0:T(8,128)(2,1)}, u32[]{:S(2)}, u32[]{:S(2)}) %all-to-all-start) | async-done | bytes 786464 | tf_op jit(solution)/shard_map/all_to_all | solution.py:110
  167.1 2.6 gather_fusion
  169.8 1.8 fusion.10
  173.4 4.0 collective-permute-start
  178.0 5.8 collective-permute-done.1
  186.8 1.7 convert_add_fusion
  188.6 3.0 reshape.169
  191.6 4.2 reduce_sum.31
  198.4 4.9 collective-permute-start.2
  210.6 2.5 reshape.170
  213.1 2.8 reduce_sum.32
  215.9 2.6 fusion.35
  220.1 1.6 fusion.31
  223.2 3.4 collective-permute-start.5
  229.8 2.9 collective-permute-done.4
  232.7 2.6 multiply_bitcast_fusion
  237.4 2.3 copy.17
  239.8 2.8 convolution_convert_fusion
  250.5 5.2 copy.29
  255.7 9.5 reshape.363
  267.1 317.6 %all-reduce.3.cloned.1.call-done = bf16[2,384,768]{2,0,1:T(2,128)(2,1)} async-done(((bf16[2,384,768]{2,0,1:T(2,128)(2,1)}), bf16[2,384,768]{2,0,1:T(2,128)(2,1)}) %all-reduce.3.cloned.1.call-update) | async-done | bytes 1179664
  586.9 243.7 %reduce-scatter.12.cloned.1.call-done = bf16[24,2048]{1,0:T(8,128)(2,1)} async-done(((bf16[768,2048]{1,0:T(8,128)(2,1)}), bf16[24,2048]{1,0:T(8,128)(2,1)}) %reduce-scatter.12.cloned.1.call-update) | async-done | bytes 98320 | tf_op jit(solution)/shard_map/reduce_scatter | solution.py:175
  830.7 229.4 %reduce-scatter.16.cloned.1.call-done = bf16[24,2304]{1,0:T(8,128)(2,1)} async-done(((bf16[768,2304]{1,0:T(8,128)(2,1)}), bf16[24,2304]{1,0:T(8,128)(2,1)}) %reduce-scatter.16.cloned.1.call-update) | async-done | bytes 110608
  1062.5 2.4 reshape.365
  1064.9 14.0 %reduce-scatter.20.cloned.1.call-done = bf16[192,24]{1,0:T(8,128)(2,1)} async-done(((bf16[768,24]{1,0:T(8,128)(2,1)}), bf16[192,24]{1,0:T(8,128)(2,1)}) %reduce-scatter.20.cloned.1.call-update) | async-done | bytes 9232
  1080.5 18.3 %reduce-scatter.14.cloned.1.call-done = bf16[24,512]{1,0:T(8,128)(2,1)} async-done(((bf16[24,2048]{1,0:T(8,128)(2,1)}), bf16[24,512]{1,0:T(8,128)(2,1)}) %reduce-scatter.14.cloned.1.call-update) | async-done | bytes 24592 | tf_op jit(solution)/shard_map/reduce_scatter | solution.py:186
  1100.2 19.0 %reduce-scatter.18.cloned.1.call-done = bf16[96,144]{1,0:T(8,128)(2,1)} async-done(((bf16[384,144]{1,0:T(8,128)(2,1)}), bf16[96,144]{1,0:T(8,128)(2,1)}) %reduce-scatter.18.cloned.1.call-update) | async-done | bytes 27664
  (164 shorter events, 45.4 us)
Async XLA Ops:
  7.2 208.8 %copy-start = (bf16[768,2048]{1,0:T(8,128)(2,1)S(1)}, bf16[768,2048]{1,0:T(8,128)(2,1)}, u32[]{:S(2)}) copy-start(bf16[768,2048]{1,0:T(8,128)(2,1)} %param.15) | copy-start | bytes 9437188
  7.2 1.5 copy-start.27
  7.2 122.4 %all-gather.2.cloned.1.call-start = ((), (), s32[]{:S(2)}) async-start(), calls=%async_computation.6 | async-start | bytes 15728640 | tf_op jit(solution)/shard_map/all_gather | solution.py:105
  143.0 24.1 %all-to-all-start = ((bf16[32,16,768]{2,1,0:T(8,128)(2,1)}), bf16[32,16,768]{2,1,0:T(8,128)(2,1)}, u32[]{:S(2)}, u32[]{:S(2)}) async-start(bf16[32,16,768]{2,1,0:T(8,128)(2,1)} %bitcast.145), calls=%async_computation | async-start | bytes 1572864 | tf_op jit(solution)/shard_map/all_to_all | solution.py:110
  152.3 432.4 %all-reduce.3.cloned.1.call-start = ((), (), s32[]{:S(2)}) async-start(), calls=%async_computation.12 | async-start | bytes 2359296
  169.7 3.1 copy-start.4
  169.8 7.6 copy-start.7
  171.5 13.7 %copy-start.5 = (bf16[512,768]{1,0:T(8,128)(2,1)}, bf16[512,768]{1,0:T(8,128)(2,1)S(1)}, u32[]{:S(2)}) copy-start(bf16[512,768]{1,0:T(8,128)(2,1)S(1)} %get-tuple-element.20) | copy-start | bytes 2359300
  171.6 12.2 %collective-permute-start.1 = (bf16[256,768]{1,0:T(8,128)(2,1)S(1)}, bf16[256,768]{1,0:T(8,128)(2,1)S(1)}, u32[]{:S(2)}, u32[]{:S(2)}) collective-permute-start(bf16[256,768]{1,0:T(8,128)(2,1)S(1)} %get-tuple-element.25), channel_id=1, source_target_pairs={{1,0},{2,1},{3,2},{4,3},{5,4},{6,5},{7,6},{8,7},{9,8},{10,9},{11,1... | collective-permute-start | bytes 1179656 | tf_op jit(solution)/shard_map/ppermute | solution.py:19
  173.4 11.8 %collective-permute-start = (bf16[256,768]{1,0:T(8,128)(2,1)S(1)}, bf16[256,768]{1,0:T(8,128)(2,1)S(1)}, u32[]{:S(2)}, u32[]{:S(2)}) collective-permute-start(bf16[256,768]{1,0:T(8,128)(2,1)S(1)} %get-tuple-element.24), channel_id=1, source_target_pairs={{0,1},{1,2},{2,3},{3,4},{4,5},{5,6},{6,7},{7,8},{8,9},{9,10},{10,1... | collective-permute-start | bytes 1179656 | tf_op jit(solution)/shard_map/ppermute | solution.py:18
  185.2 1.7 copy-start.16
  197.1 7.8 collective-permute-start.3
  198.4 8.6 collective-permute-start.2
  207.0 2.4 copy-start.2
  207.0 2.4 copy-start.17
  207.0 1.6 copy-start.21
  220.1 7.8 copy-start.9
  223.2 9.4 copy-start.3
  223.2 5.1 collective-permute-start.5
  226.6 6.0 collective-permute-start.4
  237.4 2.4 copy-start.14
  237.4 2.4 copy-start.15
  239.7 590.9 %reduce-scatter.12.cloned.1.call-start = ((), (), s32[]{:S(2)}) async-start(), calls=%async_computation.7 | async-start | bytes 3244032 | tf_op jit(solution)/shard_map/reduce_scatter | solution.py:175
  242.6 1.3 copy-start.22
  242.6 817.5 %reduce-scatter.16.cloned.1.call-start = ((), (), s32[]{:S(2)}) async-start(), calls=%async_computation.9 | async-start | bytes 3649536
  244.7 1.5 copy-start.18
  244.7 1.7 copy-start.20
  246.4 1.2 copy-start.29
  265.3 813.6 %reduce-scatter.20.cloned.1.call-start = ((), (), s32[]{:S(2)}) async-start(), calls=%async_computation.11 | async-start | bytes 245760
  586.8 512.0 %reduce-scatter.14.cloned.1.call-start = ((), (), s32[]{:S(2)}) async-start(), calls=%async_computation.8 | async-start | bytes 122880 | tf_op jit(solution)/shard_map/reduce_scatter | solution.py:186
  830.6 288.6 %reduce-scatter.18.cloned.1.call-start = ((), (), s32[]{:S(2)}) async-start(), calls=%async_computation.10 | async-start | bytes 245760
  1060.1 60.9 %copy-start.1 = (bf16[768,2048]{1,0:T(8,128)(2,1)S(1)}, bf16[768,2048]{1,0:T(8,128)(2,1)}, u32[]{:S(2)}) copy-start(bf16[768,2048]{1,0:T(8,128)(2,1)} %param.15) | copy-start | bytes 9437188
  (13 other events, 11.9 us)
Sparse Core Ops, SparseCore 0:
  9.7 119.8 all-gather.1
  239.9 344.7 all-reduce.2
  590.4 240.1 reduce-scatter.11
  836.2 223.8 reduce-scatter.15
  1062.4 16.4 reduce-scatter.19
  1081.1 17.6 reduce-scatter.13
  1101.3 17.8 reduce-scatter.17
where the time goes:
time: 1130 us
  waiting for transfers between devices  965 us (85%)
  local copies, waits for them, and re-layouts  45.9 us (4%)
  matrix products  40.8 us (4%)
  other arithmetic  34.5 us (3%)
  starting transfers between devices  25.9 us (2%)
  between operations  16.2 us (1%)
    unnamed x11, waiting for transfers between devices  581 us
    reduce_scatter x1, waiting for transfers between devices, shards(): lax.psum_scatter(readout_grad.astype(jnp.bfloat16), 'seq', scatter_dimens...  244 us
    all_gather x1, waiting for transfers between devices, shards(): lax.all_gather(projection, 'dp', axis=0, tiled=True)  98.4 us
    unnamed x76, local copies, waits for them, and re-layouts  32.6 us
  transfers between devices with their start and end apart: 14, of which 11 were waited for; matrix products, arithmetic and copies ran while one was open for 5% of the time, Pallas kernels for 0%

commit v1 on v0

--- a/solution.py
+++ b/solution.py
@@ -102,7 +102,9 @@
     outgoing = (
         jnp.dot(
             local_rows,
-            lax.all_gather(projection, "dp", axis=0, tiled=True),
+            jnp.concatenate(
+                lax.all_to_all(jnp.stack([projection] * lax.axis_size("dp")), "dp", 0, 0), axis=0
+            ),
             preferred_element_type=jnp.float32,
         )
         * inside[:, None]

time: 1130 us -> 1170 us (1.035)
  local copies, waits for them, and re-layouts: 45.9 us -> 59 us
    all_to_all x0 -> x1, waiting for transfers between devices: none -> 114 us  [shards(): lax.all_to_all(jnp.stack([projection] * lax.axis_size('dp')), 'dp', 0, 0)]
    all_gather x1 -> x0, waiting for transfers between devices: 98.4 us -> none  [shards(): lax.all_gather(projection, 'dp', axis=0, tiled=True)]
    unnamed x11 -> x10, waiting for transfers between devices: 581 us -> 580 us
    unnamed x76 -> x70, local copies, waits for them, and re-layouts: 32.6 us -> 32.3 us
  transfers between devices with their start and end apart: 14 -> 14, of which waited for: 11 -> 10; matrix products, arithmetic and copies ran while one was open for 5% -> 6% of each run, Pallas kernels for 0% -> 0%
where the time goes in v1:
time: 1170 us; the launch traced here: 1160 us
  waiting for transfers between devices  973 us (83%)
  local copies, waits for them, and re-layouts  59 us (5%)
  matrix products  46.5 us (4%)
  starting transfers between devices  35.3 us (3%)
  other arithmetic  34.4 us (3%)
  between operations  16 us (1%)
    unnamed x10, waiting for transfers between devices  580 us
    reduce_scatter x1, waiting for transfers between devices, shards(): lax.psum_scatter(readout_grad.astype(jnp.bfloat16), 'seq', scatter_dimens...  242 us
    all_to_all x1, waiting for transfers between devices, shards(): lax.all_to_all(jnp.stack([projection] * lax.axis_size('dp')), 'dp', 0, 0)  114 us
    unnamed x70, local copies, waits for them, and re-layouts  32.3 us
  transfers between devices with their start and end apart: 14, of which 10 were waited for; matrix products, arithmetic and copies ran while one was open for 6% of the time, Pallas kernels for 0%

profile of v1, /device:TPU:1, one launch (start us, length us, event | category | flops | bytes accessed | tf_op | source)
XLA Modules:
  0.0 1164.5 jit_solution(15645838161033684872)
XLA Ops:
  7.2 7.3 stack.63
  14.5 7.8 all-to-all-start
  25.5 4.4 compare_select_fusion.2
  29.9 15.5 %fusion.98 = f32[512]{0:T(512)S(1)} fusion(pred[512]{0:T(512)(128)(4,1)S(1)} %compare_reduce_fusion, pred[512]{0:T(512)(128)(4,1)S(1)} %compare_reduce_fusion.1, pred[512]{0:T(512)(128)(4,1)S(1)} %compare_reduce_fusion.2, pred[512]{0:T(512)(128)(4,1)S(1)} %compare_reduce_fusion.3, pred[512]{0:T(512)(128)(4,1)S(1)} %compare_reduce_fusion.4, ...), kind=kLoop, calls=%fused_computation.194 | loop fusion | flops 25600 | bytes 17000 | tf_op jit(solution)/shard_map/convert_element_type | solution.py:101
  45.4 114.2 %all-to-all-done = bf16[4,2048,768]{2,1,0:T(8,128)(2,1)} async-done(((bf16[4,2048,768]{2,1,0:T(8,128)(2,1)}), bf16[4,2048,768]{2,1,0:T(8,128)(2,1)}, u32[]{:S(2)}, u32[]{:S(2)}) %all-to-all-start) | async-done | bytes 12582944 | tf_op jit(solution)/shard_map/all_to_all | solution.py:106
  159.6 13.4 %fusion.13 = bf16[512,768]{1,0:T(8,128)(2,1)} fusion(bf16[8192,768]{1,0:T(8,128)(2,1)} %bitcast.1, bf16[1,1,512,8192]{3,2,1,0:T(8,128)(2,1)} %param.8, f32[512]{0:T(512)S(1)} %fusion.98), kind=kOutput, calls=%fused_computation.29 | convolution fusion | flops 6443237376 | bytes 21760000 | tf_op jit(solution)/shard_map/dot_general | solution.py:103
  173.1 10.7 all-to-all-start.1
  184.1 13.5 %all-to-all-done.1 = bf16[32,16,768]{2,1,0:T(8,128)(2,1)} async-done(((bf16[32,16,768]{2,1,0:T(8,128)(2,1)}), bf16[32,16,768]{2,1,0:T(8,128)(2,1)}, u32[]{:S(2)}, u32[]{:S(2)}) %all-to-all-start.1) | async-done | bytes 786464 | tf_op jit(solution)/shard_map/all_to_all | solution.py:112
  197.7 2.6 gather_fusion
  203.9 4.2 collective-permute-start
  208.7 3.4 collective-permute-done.1
  216.9 3.0 reshape.175
  219.9 4.2 reduce_sum.31
  226.7 4.7 collective-permute-start.2
  238.6 2.5 reshape.176
  241.1 2.8 reduce_sum.32
  243.9 2.6 fusion.35
  253.9 3.5 collective-permute-start.5
  262.8 2.6 multiply_bitcast_fusion
  266.7 2.9 reshape.178
  269.6 2.0 fusion.24
  271.7 2.3 copy.17
  274.1 3.9 convolution_convert_fusion
  287.2 5.2 copy.29
  292.4 9.5 reshape.369
  303.8 317.6 %all-reduce.3.cloned.1.call-done = bf16[2,384,768]{2,0,1:T(2,128)(2,1)} async-done(((bf16[2,384,768]{2,0,1:T(2,128)(2,1)}), bf16[2,384,768]{2,0,1:T(2,128)(2,1)}) %all-reduce.3.cloned.1.call-update) | async-done | bytes 1179664
  625.0 242.4 %reduce-scatter.12.cloned.1.call-done = bf16[24,2048]{1,0:T(8,128)(2,1)} async-done(((bf16[768,2048]{1,0:T(8,128)(2,1)}), bf16[24,2048]{1,0:T(8,128)(2,1)}) %reduce-scatter.12.cloned.1.call-update) | async-done | bytes 98320 | tf_op jit(solution)/shard_map/reduce_scatter | solution.py:177
  867.4 229.6 %reduce-scatter.16.cloned.1.call-done = bf16[24,2304]{1,0:T(8,128)(2,1)} async-done(((bf16[768,2304]{1,0:T(8,128)(2,1)}), bf16[24,2304]{1,0:T(8,128)(2,1)}) %reduce-scatter.16.cloned.1.call-update) | async-done | bytes 110608
  1099.2 2.4 reshape.371
  1101.7 14.1 %reduce-scatter.20.cloned.1.call-done = bf16[192,24]{1,0:T(8,128)(2,1)} async-done(((bf16[768,24]{1,0:T(8,128)(2,1)}), bf16[192,24]{1,0:T(8,128)(2,1)}) %reduce-scatter.20.cloned.1.call-update) | async-done | bytes 9232
  1117.4 18.3 %reduce-scatter.14.cloned.1.call-done = bf16[24,512]{1,0:T(8,128)(2,1)} async-done(((bf16[24,2048]{1,0:T(8,128)(2,1)}), bf16[24,512]{1,0:T(8,128)(2,1)}) %reduce-scatter.14.cloned.1.call-update) | async-done | bytes 24592 | tf_op jit(solution)/shard_map/reduce_scatter | solution.py:188
  1137.0 18.9 %reduce-scatter.18.cloned.1.call-done = bf16[96,144]{1,0:T(8,128)(2,1)} async-done(((bf16[384,144]{1,0:T(8,128)(2,1)}), bf16[96,144]{1,0:T(8,128)(2,1)}) %reduce-scatter.18.cloned.1.call-update) | async-done | bytes 27664
  (158 shorter events, 56.3 us)
Async XLA Ops:
  7.2 236.8 %copy-start = (bf16[768,2048]{1,0:T(8,128)(2,1)S(1)}, bf16[768,2048]{1,0:T(8,128)(2,1)}, u32[]{:S(2)}) copy-start(bf16[768,2048]{1,0:T(8,128)(2,1)} %param.15) | copy-start | bytes 9437188
  14.5 8.5 copy-start.24
  14.5 145.1 %all-to-all-start = ((bf16[4,2048,768]{2,1,0:T(8,128)(2,1)}), bf16[4,2048,768]{2,1,0:T(8,128)(2,1)}, u32[]{:S(2)}, u32[]{:S(2)}) async-start(bf16[4,2048,768]{2,1,0:T(8,128)(2,1)} %stack.63), calls=%async_computation | async-start | bytes 25165824 | tf_op jit(solution)/shard_map/all_to_all | solution.py:106
  173.1 24.6 %all-to-all-start.1 = ((bf16[32,16,768]{2,1,0:T(8,128)(2,1)}), bf16[32,16,768]{2,1,0:T(8,128)(2,1)}, u32[]{:S(2)}, u32[]{:S(2)}) async-start(bf16[32,16,768]{2,1,0:T(8,128)(2,1)} %bitcast.146), calls=%async_computation.1 | async-start | bytes 1572864 | tf_op jit(solution)/shard_map/all_to_all | solution.py:112
  183.8 437.7 %all-reduce.3.cloned.1.call-start = ((), (), s32[]{:S(2)}) async-start(), calls=%async_computation.12 | async-start | bytes 2359296
  200.3 3.1 copy-start.5
  200.3 7.8 copy-start.8
  202.1 11.4 copy-start.6
  202.1 10.0 collective-permute-start.1
  203.9 9.6 collective-permute-start
  213.5 1.7 copy-start.16
  225.4 7.5 collective-permute-start.3
  226.7 8.3 collective-permute-start.2
  235.0 2.4 copy-start.1
  235.0 2.4 copy-start.17
  235.0 1.6 copy-start.20
  250.6 8.3 copy-start.10
  250.6 8.3 copy-start.11
  252.4 10.4 copy-start.3
  253.9 8.9 copy-start.2
  253.9 6.2 collective-permute-start.5
  257.4 5.4 collective-permute-start.4
  269.6 2.0 copy-start.14
  274.0 593.3 %reduce-scatter.12.cloned.1.call-start = ((), (), s32[]{:S(2)}) async-start(), calls=%async_computation.7 | async-start | bytes 3244032 | tf_op jit(solution)/shard_map/reduce_scatter | solution.py:177
  278.0 819.0 %reduce-scatter.16.cloned.1.call-start = ((), (), s32[]{:S(2)}) async-start(), calls=%async_computation.9 | async-start | bytes 3649536
  278.1 2.9 copy-start.4
  281.4 1.5 copy-start.18
  281.4 1.7 copy-start.19
  283.1 1.2 copy-start.26
  302.0 813.8 %reduce-scatter.20.cloned.1.call-start = ((), (), s32[]{:S(2)}) async-start(), calls=%async_computation.11 | async-start | bytes 245760
  624.9 510.7 %reduce-scatter.14.cloned.1.call-start = ((), (), s32[]{:S(2)}) async-start(), calls=%async_computation.8 | async-start | bytes 122880 | tf_op jit(solution)/shard_map/reduce_scatter | solution.py:188
  867.4 288.6 %reduce-scatter.18.cloned.1.call-start = ((), (), s32[]{:S(2)}) async-start(), calls=%async_computation.10 | async-start | bytes 245760
  (10 other events, 8.9 us)
Sparse Core Ops, SparseCore 0:
  274.2 347.2 all-reduce.2
  627.2 240.1 reduce-scatter.11
  873.1 223.8 reduce-scatter.15
  1099.3 16.3 reduce-scatter.19
  1117.9 17.6 reduce-scatter.13
  1138.0 17.8 reduce-scatter.17
